TPU v7x, 256 devices: a whole 4x4x8 slice. The times are simulated.
256 devices in a mesh: acq: 32 (over z, x), rows: 8 (over y, core).
Axes of the slice: x: 4, y: 4, z: 8, core: 2. Of those that a mesh axis runs over, the one named last changes fastest.
Arguments:
- slc: bfloat16 [2, 32, 640, 5120], P(None, 'acq', 'rows'), may hold values from -600 to 600, as said below
- validity: int32 [32, 10], P('acq'), may hold values 0 or 1
Outputs:
- coherence: float32 [2, 128, 256, 320], P(None, None, ('acq', 'rows'))
Inputs may be any that keep to these rules, and one draw needn't show every extreme that they name: `slc`: finite values.
All inputs are finite; a program needn't handle non-finite values. No bound on the sum of `validity` on one device may be relied on, other than what follows from the above.
Results may differ from a plain program's by a relative error of at most 0.0003.
Values may be sent and summed in bfloat16 or wider, within the bound.
A program may use at most 128 MiB of HBM per device.

v0:
```python
import jax
import jax.numpy as jnp
from jax import lax
from jax.sharding import PartitionSpec as P

ACQ_DEV = 1
PARTNERS = 10
AZ_LOOKS = 5
RG_LOOKS = 20


EPS = 1e-06


def passed_along(array, axis, by):
    peers = lax.axis_size(axis)
    pairs = [(i, i + by) for i in range(peers) if 0 <= i + by < peers]
    return lax.ppermute(array, axis, pairs)


def box_tables(rows, cols):
    look_rows = rows // AZ_LOOKS
    look_cols = cols // RG_LOOKS
    col_table = (
        lax.broadcasted_iota(jnp.int32, (cols, look_cols), 0) // RG_LOOKS
        == lax.broadcasted_iota(jnp.int32, (cols, look_cols), 1)
    ).astype(jnp.float32)
    row_table = (
        lax.broadcasted_iota(jnp.int32, (look_rows, rows), 1) // AZ_LOOKS
        == lax.broadcasted_iota(jnp.int32, (look_rows, rows), 0)
    ).astype(jnp.float32)
    return (row_table, col_table)


def box_mean(values):
    count, rows, cols = values.shape
    row_table, col_table = box_tables(rows, cols)
    across = jnp.dot(
        values.reshape(count * rows, cols),
        col_table,
        precision=lax.Precision.HIGHEST,
        preferred_element_type=jnp.float32,
    )
    across = across.reshape(count, rows, cols // RG_LOOKS)
    summed = jnp.einsum(
        "ur,nrv->nuv",
        row_table,
        across,
        precision=lax.Precision.HIGHEST,
        preferred_element_type=jnp.float32,
    )
    return summed / (AZ_LOOKS * RG_LOOKS)


def coherence_block(extended, allowed):
    count = allowed.shape[0]
    real_all = extended[0]
    imag_all = extended[1]
    power = box_mean(
        jnp.square(real_all.astype(jnp.float32)) + jnp.square(imag_all.astype(jnp.float32))
    )
    lead_power = power[:count]
    lead_re_half = real_all[:count]
    lead_im_half = imag_all[:count]

    def one_offset(offset):
        later_re = lax.dynamic_slice_in_dim(real_all, offset, count, 0).astype(jnp.float32)
        later_im = lax.dynamic_slice_in_dim(imag_all, offset, count, 0).astype(jnp.float32)
        lead_re = lead_re_half.astype(jnp.float32)
        lead_im = lead_im_half.astype(jnp.float32)
        cross_re = box_mean(lead_re * later_re + lead_im * later_im)
        cross_im = box_mean(lead_im * later_re - lead_re * later_im)
        later_power = lax.dynamic_slice_in_dim(power, offset, count, 0)
        scale = lax.rsqrt((lead_power + EPS) * (later_power + EPS))
        column = lax.dynamic_slice_in_dim(allowed, offset - 1, 1, 1)
        weight = scale * column[:, :, None]
        return jnp.stack([cross_re * weight, cross_im * weight])

    stacked = lax.map(one_offset, jnp.arange(1, PARTNERS + 1, dtype=jnp.int32))
    looks_r = stacked.shape[3]
    looks_c = stacked.shape[4]
    return stacked.transpose(1, 3, 4, 2, 0).reshape(2, looks_r, looks_c, count * PARTNERS)


def allowed_pairs(validity, first, total):
    count = validity.shape[0]
    offsets = jnp.arange(1, PARTNERS + 1, dtype=jnp.int32)[None, :]
    position = first + jnp.arange(count, dtype=jnp.int32)[:, None]
    return ((validity > 0) & (position + offsets < total)).astype(jnp.float32)


def per_device(slc, validity):
    reach = -(-PARTNERS // ACQ_DEV)
    pieces = [slc]
    for distance in range(1, reach + 1):
        pieces.append(passed_along(slc, "acq", -distance))
    extended = jnp.concatenate(pieces, axis=1)
    total = lax.axis_size("acq") * ACQ_DEV
    first = lax.axis_index("acq") * ACQ_DEV
    allowed = allowed_pairs(validity, first, total)
    local = coherence_block(extended, allowed)
    return lax.all_to_all(
        lax.all_to_all(local, "acq", split_axis=2, concat_axis=3, tiled=True),
        "rows",
        split_axis=2,
        concat_axis=1,
        tiled=True,
    )


def solution(mesh):
    in_specs = (P(None, "acq", "rows", None), P("acq", None))
    out_specs = P(None, None, ("acq", "rows"), None)
    return jax.shard_map(
        per_device, mesh=mesh, in_specs=in_specs, out_specs=out_specs, check_vma=False
    )
```

profile of v0, /device:TPU:33, one launch (start us, length us, event | category | flops | bytes accessed | tf_op | source)
XLA Modules:
  0.0 967.2 jit_solution(4580933812872670297)
XLA Ops:
  0.0 4.1 collective-permute-start
  4.1 2.4 collective-permute-start.1
  6.5 1.9 collective-permute-start.2
  8.4 1.9 collective-permute-start.3
  11.7 2.7 slice_bitcast_fusion.2
  16.6 57.5 %collective-permute-done = bf16[2,1,80,5120]{3,2,1,0:T(8,128)(2,1)} collective-permute-done((bf16[2,1,80,5120]{3,2,1,0:T(8,128)(2,1)}, bf16[2,1,80,5120]{3,2,1,0:T(8,128)(2,1)}, u32[]{:S(2)}, u32[]{:S(2)}) %collective-permute-start) | collective-permute-done | bytes 1638432 | tf_op jit(solution)/shard_map/ppermute | solution.py:18
  75.4 1.5 constant_dynamic-update-slice_fusion.9
  77.0 57.5 %collective-permute-done.1 = bf16[2,1,80,5120]{3,2,1,0:T(8,128)(2,1)} collective-permute-done((bf16[2,1,80,5120]{3,2,1,0:T(8,128)(2,1)}, bf16[2,1,80,5120]{3,2,1,0:T(8,128)(2,1)}, u32[]{:S(2)}, u32[]{:S(2)}) %collective-permute-start.1) | collective-permute-done | bytes 1638432 | tf_op jit(solution)/shard_map/ppermute | solution.py:18
  135.8 1.5 constant_dynamic-update-slice_fusion.8
  137.3 33.1 %collective-permute-done.2 = bf16[2,1,80,5120]{3,2,1,0:T(8,128)(2,1)} collective-permute-done((bf16[2,1,80,5120]{3,2,1,0:T(8,128)(2,1)}, bf16[2,1,80,5120]{3,2,1,0:T(8,128)(2,1)}, u32[]{:S(2)}, u32[]{:S(2)}) %collective-permute-start.2) | collective-permute-done | bytes 1638432 | tf_op jit(solution)/shard_map/ppermute | solution.py:18
  171.7 1.5 constant_dynamic-update-slice_fusion.7
  173.2 34.7 %collective-permute-done.3 = bf16[2,1,80,5120]{3,2,1,0:T(8,128)(2,1)} collective-permute-done((bf16[2,1,80,5120]{3,2,1,0:T(8,128)(2,1)}, bf16[2,1,80,5120]{3,2,1,0:T(8,128)(2,1)}, u32[]{:S(2)}, u32[]{:S(2)}) %collective-permute-start.3) | collective-permute-done | bytes 1638432 | tf_op jit(solution)/shard_map/ppermute | solution.py:18
  209.2 1.5 constant_dynamic-update-slice_fusion.6
  212.3 13.5 %collective-permute-done.6 = bf16[2,1,80,5120]{3,2,1,0:T(8,128)(2,1)S(1)} collective-permute-done((bf16[2,1,80,5120]{3,2,1,0:T(8,128)(2,1)S(1)}, bf16[2,1,80,5120]{3,2,1,0:T(8,128)(2,1)S(1)}, u32[]{:S(2)}, u32[]{:S(2)}) %collective-permute-start.6) | collective-permute-done | bytes 1638432 | tf_op jit(solution)/shard_map/ppermute | solution.py:18
  225.8 404.2 %collective-permute-done.7 = bf16[2,1,80,5120]{3,2,1,0:T(8,128)(2,1)S(1)} collective-permute-done((bf16[2,1,80,5120]{3,2,1,0:T(8,128)(2,1)S(1)}, bf16[2,1,80,5120]{3,2,1,0:T(8,128)(2,1)S(1)}, u32[]{:S(2)}, u32[]{:S(2)}) %collective-permute-start.7) | collective-permute-done | bytes 1638432 | tf_op jit(solution)/shard_map/ppermute | solution.py:18
  630.4 7.4 slice_bitcast_fusion
  637.8 4.2 copy-done
  642.0 18.2 %fusion.36 = f32[11,80,256]{2,1,0:T(8,128)S(1)} fusion(s32[5120]{0:T(1024)S(1)} %get-tuple-element.265, s32[5120]{0:T(1024)S(1)} %get-tuple-element.266, pred[5120]{0:T(1024)(128)(4,1)S(1)} %fusion.50, bf16[2,11,80,5120]{3,2,1,0:T(8,128)(2,1)} %copy-done), kind=kOutput, calls=%fused_computation.54 | convolution fusion | flops 13866352640 | bytes 18969600 | tf_op jit(solution)/shard_map/dot_general | solution.py:38
  660.7 151.3 %while.15 = (s32[]{:T(128)}, f32[10,2,1,16,256]{4,3,1,2,0:T(8,128)S(1)}, bf16[1,80,5120]{2,1,0:T(8,128)(2,1)S(1)}, s32[10]{0:T(128)S(1)}, bf16[11,80,5120]{2,1,0...) while((s32[]{:T(128)}, ...), condition=%wide.region_1.2_spmd, body=%wide.region_0.1_spmd.sunk | while | flops 2535522816 | bytes 7185793 | solution.py:79
  663.3 4.5 fusion.76
  670.5 4.5 fusion.74
  678.4 4.5 fusion.76
  685.6 4.5 fusion.74
  693.5 4.5 fusion.76
  700.7 4.5 fusion.74
  708.7 4.5 fusion.76
  715.9 4.5 fusion.74
  723.8 4.5 fusion.76
  731.0 4.5 fusion.74
  738.9 4.5 fusion.76
  746.1 4.5 fusion.74
  754.1 4.5 fusion.76
  761.3 4.5 fusion.74
  769.2 4.5 fusion.76
  776.4 4.5 fusion.74
  784.3 4.5 fusion.76
  791.5 4.5 fusion.74
  799.4 4.5 fusion.76
  806.7 4.5 fusion.74
  812.0 1.6 copy.10
  813.6 2.4 bitcast_bitcast_fusion
  816.0 5.2 reshape.114
  821.2 110.9 %all_to_all.36 = f32[32,1,2560]{2,1,0:T(1,128)S(1)} all-to-all(f32[32,1,2560]{2,1,0:T(1,128)S(1)} %reshape.114), channel_id=1, replica_groups=mesh['acq'=32,'rows'=8] {'acq'}, dimensions={0} | all-to-all | bytes 655360 | tf_op jit(solution)/shard_map/all_to_all | solution.py:103
  934.1 3.5 reshape.115
  937.5 1.8 copy.19
  939.4 6.1 copy.16
  945.5 4.7 reshape.113
  950.2 16.1 %all_to_all.37 = f32[2,16,8,320]{3,1,0,2:T(8,128)S(1)} all-to-all(f32[2,16,8,320]{3,1,0,2:T(8,128)S(1)} %reshape.113), channel_id=1, replica_groups=mesh['acq'=32,'rows'=8] {'rows'}, dimensions={2} | all-to-all | bytes 655360 | tf_op jit(solution)/shard_map/all_to_all | solution.py:102
  (129 shorter events, 41.8 us)
Async XLA Ops:
  0.0 74.1 %copy-start.1 = (bf16[2,1,80,5120]{3,2,1,0:T(8,128)(2,1)S(1)}, bf16[2,1,80,5120]{3,2,1,0:T(8,128)(2,1)}, u32[]{:S(2)}) copy-start(bf16[2,1,80,5120]{3,2,1,0:T(8,128)(2,1)} %param.4) | copy-start | bytes 4915204
  0.0 74.1 %collective-permute-start = (bf16[2,1,80,5120]{3,2,1,0:T(8,128)(2,1)}, bf16[2,1,80,5120]{3,2,1,0:T(8,128)(2,1)}, u32[]{:S(2)}, u32[]{:S(2)}) collective-permute-start(bf16[2,1,80,5120]{3,2,1,0:T(8,128)(2,1)} %param.4), channel_id=1, source_target_pairs={{8,0},{16,8},{24,16},{32,24},{40,32},{48,40},{56,48},{64,56},{72,6... | collective-permute-start | bytes 4915208 | tf_op jit(solution)/shard_map/ppermute | solution.py:18
  4.1 130.4 %collective-permute-start.1 = (bf16[2,1,80,5120]{3,2,1,0:T(8,128)(2,1)}, bf16[2,1,80,5120]{3,2,1,0:T(8,128)(2,1)}, u32[]{:S(2)}, u32[]{:S(2)}) collective-permute-start(bf16[2,1,80,5120]{3,2,1,0:T(8,128)(2,1)} %param.4), channel_id=1, source_target_pairs={{16,0},{24,8},{32,16},{40,24},{48,32},{56,40},{64,48},{72,56},{80,... | collective-permute-start | bytes 4915208 | tf_op jit(solution)/shard_map/ppermute | solution.py:18
  6.5 163.9 %collective-permute-start.2 = (bf16[2,1,80,5120]{3,2,1,0:T(8,128)(2,1)}, bf16[2,1,80,5120]{3,2,1,0:T(8,128)(2,1)}, u32[]{:S(2)}, u32[]{:S(2)}) collective-permute-start(bf16[2,1,80,5120]{3,2,1,0:T(8,128)(2,1)} %param.4), channel_id=1, source_target_pairs={{24,0},{32,8},{40,16},{48,24},{56,32},{64,40},{72,48},{80,56},{88,... | collective-permute-start | bytes 4915208 | tf_op jit(solution)/shard_map/ppermute | solution.py:18
  8.4 199.4 %collective-permute-start.3 = (bf16[2,1,80,5120]{3,2,1,0:T(8,128)(2,1)}, bf16[2,1,80,5120]{3,2,1,0:T(8,128)(2,1)}, u32[]{:S(2)}, u32[]{:S(2)}) collective-permute-start(bf16[2,1,80,5120]{3,2,1,0:T(8,128)(2,1)} %param.4), channel_id=1, source_target_pairs={{32,0},{40,8},{48,16},{56,24},{64,32},{72,40},{80,48},{88,56},{96,... | collective-permute-start | bytes 4915208 | tf_op jit(solution)/shard_map/ppermute | solution.py:18
  10.4 200.3 %collective-permute-start.4 = (bf16[2,1,80,5120]{3,2,1,0:T(8,128)(2,1)}, bf16[2,1,80,5120]{3,2,1,0:T(8,128)(2,1)S(1)}, u32[]{:S(2)}, u32[]{:S(2)}) collective-permute-start(bf16[2,1,80,5120]{3,2,1,0:T(8,128)(2,1)} %param.4), channel_id=1, source_target_pairs={{40,0},{48,8},{56,16},{64,24},{72,32},{80,40},{88,48},{96,56},{104... | collective-permute-start | bytes 4915208 | tf_op jit(solution)/shard_map/ppermute | solution.py:18
  74.1 138.0 %collective-permute-start.5 = (bf16[2,1,80,5120]{3,2,1,0:T(8,128)(2,1)S(1)}, bf16[2,1,80,5120]{3,2,1,0:T(8,128)(2,1)S(1)}, u32[]{:S(2)}, u32[]{:S(2)}) collective-permute-start(bf16[2,1,80,5120]{3,2,1,0:T(8,128)(2,1)S(1)} %copy-done.1), channel_id=1, source_target_pairs={{48,0},{56,8},{64,16},{72,24},{80,32},{88,40},{96,48},{104,56},{11... | collective-permute-start | bytes 4915208 | tf_op jit(solution)/shard_map/ppermute | solution.py:18
  134.5 91.2 %collective-permute-start.6 = (bf16[2,1,80,5120]{3,2,1,0:T(8,128)(2,1)S(1)}, bf16[2,1,80,5120]{3,2,1,0:T(8,128)(2,1)S(1)}, u32[]{:S(2)}, u32[]{:S(2)}) collective-permute-start(bf16[2,1,80,5120]{3,2,1,0:T(8,128)(2,1)S(1)} %copy-done.1), channel_id=1, source_target_pairs={{56,0},{64,8},{72,16},{80,24},{88,32},{96,40},{104,48},{112,56},{1... | collective-permute-start | bytes 4915208 | tf_op jit(solution)/shard_map/ppermute | solution.py:18
  170.4 459.7 %collective-permute-start.7 = (bf16[2,1,80,5120]{3,2,1,0:T(8,128)(2,1)S(1)}, bf16[2,1,80,5120]{3,2,1,0:T(8,128)(2,1)S(1)}, u32[]{:S(2)}, u32[]{:S(2)}) collective-permute-start(bf16[2,1,80,5120]{3,2,1,0:T(8,128)(2,1)S(1)} %copy-done.1), channel_id=1, source_target_pairs={{64,0},{72,8},{80,16},{88,24},{96,32},{104,40},{112,48},{120,56},{... | collective-permute-start | bytes 4915208 | tf_op jit(solution)/shard_map/ppermute | solution.py:18
  207.9 422.3 %collective-permute-start.8 = (bf16[2,1,80,5120]{3,2,1,0:T(8,128)(2,1)S(1)}, bf16[2,1,80,5120]{3,2,1,0:T(8,128)(2,1)S(1)}, u32[]{:S(2)}, u32[]{:S(2)}) collective-permute-start(bf16[2,1,80,5120]{3,2,1,0:T(8,128)(2,1)S(1)} %copy-done.1), channel_id=1, source_target_pairs={{72,0},{80,8},{88,16},{96,24},{104,32},{112,40},{120,48},{128,56},... | collective-permute-start | bytes 4915208 | tf_op jit(solution)/shard_map/ppermute | solution.py:18
  210.7 419.6 %collective-permute-start.9 = (bf16[2,1,80,5120]{3,2,1,0:T(8,128)(2,1)S(1)}, bf16[2,1,80,5120]{3,2,1,0:T(8,128)(2,1)S(1)}, u32[]{:S(2)}, u32[]{:S(2)}) collective-permute-start(bf16[2,1,80,5120]{3,2,1,0:T(8,128)(2,1)S(1)} %copy-done.1), channel_id=1, source_target_pairs={{80,0},{88,8},{96,16},{104,24},{112,32},{120,40},{128,48},{136,56}... | collective-permute-start | bytes 4915208 | tf_op jit(solution)/shard_map/ppermute | solution.py:18
  630.4 11.6 %copy-start = (bf16[2,11,80,5120]{3,2,1,0:T(8,128)(2,1)}, bf16[2,11,80,5120]{3,2,1,0:T(8,128)(2,1)S(1)}, u32[]{:S(2)}) copy-start(bf16[2,11,80,5120]{3,2,1,0:T(8,128)(2,1)S(1)} %constant_dynamic-update-slice_fusion) | copy-start | bytes 54067204
  642.0 18.7 %copy-start.2 = (bf16[1,80,5120]{2,1,0:T(8,128)(2,1)S(1)}, bf16[1,80,5120]{2,1,0:T(8,128)(2,1)}, u32[]{:S(2)}) copy-start(bf16[1,80,5120]{2,1,0:T(8,128)(2,1)} %get-tuple-element.343) | copy-start | bytes 2457604
  642.0 18.7 %copy-start.3 = (bf16[1,80,5120]{2,1,0:T(8,128)(2,1)S(1)}, bf16[1,80,5120]{2,1,0:T(8,128)(2,1)}, u32[]{:S(2)}) copy-start(bf16[1,80,5120]{2,1,0:T(8,128)(2,1)} %get-tuple-element.340) | copy-start | bytes 2457604
  642.0 18.7 %copy-start.4 = (f32[10,2,1,16,256]{4,3,1,2,0:T(8,128)S(1)}, f32[10,2,1,16,256]{4,3,1,2,0:T(8,128)}, u32[]{:S(2)}) copy-start(f32[10,2,1,16,256]{4,3,1,2,0:T(8,128)} %custom-call.1) | copy-start | bytes 983044
where the time goes:
time: 971 us; the launch traced here: 967 us
  waiting for transfers between devices  600 us (62%)
  blocking collectives  127 us (13%)
  matrix products  125 us (13%)
  local copies, waits for them, and re-layouts  61 us (6%)
  loops' own time  33 us (3%)
  starting transfers between devices  18 us (2%)
    ppermute x10, waiting for transfers between devices, passed_along(): return lax.ppermute(array, axis, pairs)  600 us
    all_to_all x1, blocking collectives, per_device(): lax.all_to_all(local, 'acq', split_axis=2, concat_axis=3, tiled=True)  111 us
    dot_general x21, matrix products, box_mean(): jnp.dot(values.reshape(count * rows, cols), col_table, precision=lax.Prec...  109 us
    another operation x1, loops' own time, coherence_block(): stacked = lax.map(one_offset, jnp.arange(1, PARTNERS + 1, dtype=jnp.int32))  33 us
    unnamed x23, local copies, waits for them, and re-layouts  23.5 us
  transfers between devices with their start and end apart: 10, of which 6 were waited for; matrix products, arithmetic and copies ran while one was open for 1% of the time, Pallas kernels for 0%

commit v1 on v0

v1 whole, which is shorter than its diff:
```python
import jax
import jax.numpy as jnp
from jax import lax
from jax.sharding import PartitionSpec as P
from jax.experimental import pallas as pl
from jax.experimental.pallas import tpu as pltpu

PARTNERS = 10
EPS = 1e-06
CELLS = 100.0
ACQ = 32
NX = 4
NZ = 8
BLOCK = 640
SLAB = 200
POWER_AT = ACQ * PARTNERS
SUMS = 384
MESH = pl.DeviceIdType.MESH
F32 = jnp.float32
BF16 = jnp.bfloat16


def z_offset(step):
    half = (step + 1) // 2
    return jnp.where(step % 2 == 1, half, lax.rem(NZ - half, NZ))


def z_position(offset):
    return jnp.where(offset <= 4, jnp.maximum(2 * offset - 1, 0), 2 * (NZ - offset))


def row_table():
    pieces = []
    for g in range(NX):
        q = lax.broadcasted_iota(jnp.int32, (40, 160), 0)
        take = ((q >> 2) & 1) * 80 + (4 * g + (q & 3)) * 5 + (q >> 3)
        pieces.append((lax.broadcasted_iota(jnp.int32, (40, 160), 1) == take).astype(F32))
    return jnp.concatenate(pieces, axis=0).astype(BF16)


def column_table():
    c = lax.broadcasted_iota(jnp.int32, (BLOCK, BLOCK), 1)
    take = (c & 31) * 20 + (c >> 7) * 4 + ((c >> 5) & 3)
    return (lax.broadcasted_iota(jnp.int32, (BLOCK, BLOCK), 0) == take).astype(F32).astype(BF16)


def kernel(
    slc_ref, validity_ref, out_ref,
    image, table, outgoing, arrived, lead, turned, sums, dense, message, received,
    own_valid, all_valid, power,
    in_sem, self_sem, send_sem, recv_sem, vsend_sem, vrecv_sem, send2_sem, recv2_sem,
):
    acq = lax.axis_index("acq")
    band = lax.axis_index("rows")
    z = acq // NX
    x = lax.rem(acq, NX)

    def z_at(step):
        return lax.rem(z + z_offset(step), NZ)

    def send_step(n):
        return lax.rem(n + 1, NZ)

    def load_block(n):
        at = pl.multiple_of(z_at(send_step(n)) * BLOCK, 128)
        return pltpu.make_async_copy(
            slc_ref.at[:, 0, :, pl.ds(at, BLOCK)], image.at[n], in_sem.at[n]
        )

    for n in range(NZ):
        load_block(n).start()

    barrier = pltpu.get_barrier_semaphore()

    def greet_acq(s, c):
        pl.semaphore_signal(
            barrier, inc=1, device_id=(lax.rem(acq + s, ACQ), band), device_id_type=MESH
        )
        return c

    lax.fori_loop(1, ACQ, greet_acq, 0)

    def greet_plane(s, c):
        pl.semaphore_signal(
            barrier,
            inc=1,
            device_id=(z * NX + s % NX, lax.rem(band + s // NX, 8)),
            device_id_type=MESH,
        )
        return c

    lax.fori_loop(NX, ACQ, greet_plane, 0)

    own_valid[...] = jnp.zeros_like(own_valid)
    own_valid[:, 0:PARTNERS] = (validity_ref[...] > 0).astype(F32)
    rows = row_table()
    table[...] = column_table()

    def prepare(n):
        load_block(n).wait()
        block = image[n].reshape(160, BLOCK)
        ordered = jnp.dot(rows, block, preferred_element_type=F32).astype(BF16)
        slab = jnp.dot(ordered, table[...], preferred_element_type=F32).astype(BF16)
        for g in range(NX):
            for c in range(5):
                outgoing[n, g, c * 40 : (c + 1) * 40, :] = slab[
                    g * 40 : (g + 1) * 40, c * 128 : (c + 1) * 128
                ]

    def slab_copy(n, g):
        return pltpu.make_async_remote_copy(
            src_ref=outgoing.at[n, g],
            dst_ref=arrived.at[acq],
            send_sem=send_sem.at[n, g],
            recv_sem=recv_sem.at[acq],
            device_id=(z_at(send_step(n)) * NX + g, band),
            device_id_type=MESH,
        )

    def valid_copy(to):
        return pltpu.make_async_remote_copy(
            src_ref=own_valid,
            dst_ref=all_valid.at[acq],
            send_sem=vsend_sem.at[to],
            recv_sem=vrecv_sem.at[acq],
            device_id=(to, band),
            device_id_type=MESH,
        )

    self_copy = pltpu.make_async_copy(outgoing.at[NZ - 1, x], arrived.at[acq], self_sem)

    def send(n):
        for g in range(NX):
            to = z_at(send_step(n)) * NX + g

            @pl.when(to != acq)
            def _():
                slab_copy(n, g).start()

    prepare(0)
    pl.semaphore_wait(barrier, 59)

    def prepare_and_send(n, c):
        send(n - 1)
        prepare(n)
        return c

    lax.fori_loop(1, NZ, prepare_and_send, 0)
    send(NZ - 1)
    self_copy.start()

    def send_valid(s, c):
        valid_copy(lax.rem(acq + s, ACQ)).start()
        return c

    lax.fori_loop(1, ACQ, send_valid, 0)

    for part in range(2):
        for k in range(1, PARTNERS + 1):
            sums[part, (k - 1) * ACQ + ACQ - k : k * ACQ] = jnp.zeros((k, 8, 128), F32)

    sublane = lax.broadcasted_iota(jnp.int32, (8, 128), 0)
    lane = lax.broadcasted_iota(jnp.int32, (8, 128), 1)
    upper = sublane < 4
    sign = jnp.where(upper, -1.0, 1.0).astype(F32)

    def slab_arrival(i):
        return pltpu.make_async_remote_copy(
            src_ref=outgoing.at[0, 0],
            dst_ref=arrived.at[i],
            send_sem=send_sem.at[0, 0],
            recv_sem=recv_sem.at[i],
            device_id=(acq, band),
            device_id_type=MESH,
        )

    def widen(i):
        for t in range(25):
            at = pl.ds(t * 8, 8)
            value = arrived[i, at, :].astype(F32)
            lead[i, at, :] = value
            turned[i, at, :] = pltpu.roll(value, 4, 0) * sign

    def pair_sums(za, gap):
        pairs = [
            (xa, xb)
            for xa in range(NX)
            for xb in range(NX)
            if 1 <= gap * NX + xb - xa <= PARTNERS
        ]
        powers = range(NX) if gap == 0 else ()

        def body(c, carry):
            carry = list(carry)
            for r in range(5):
                at = pl.ds(pl.multiple_of(c * 40 + r * 8, 8), 8)
                first = [lead[za * NX + i, at, :] for i in range(NX)]
                later = [lead[(za + gap) * NX + i, at, :] for i in range(NX)]
                later_turned = [turned[(za + gap) * NX + i, at, :] for i in range(NX)]
                m = 0
                for xa, xb in pairs:
                    carry[m] = carry[m] + first[xa] * later[xb]
                    carry[m + 1] = carry[m + 1] + first[xa] * later_turned[xb]
                    m += 2
                for i in powers:
                    carry[m] = carry[m] + first[i] * first[i]
                    m += 1
            return tuple(carry)

        zero = jnp.zeros((8, 128), F32)
        total = lax.fori_loop(0, 5, body, (zero,) * (2 * len(pairs) + len(powers)))
        m = 0
        for xa, xb in pairs:
            k = gap * NX + xb - xa
            slot = (k - 1) * ACQ + za * NX + xa
            sums[0, slot] = total[m]
            sums[1, slot] = total[m + 1]
            m += 2
        for i in powers:
            sums[0, POWER_AT + za * NX + i] = total[m]
            m += 1

    def arrival(step, carry):
        zn = z_at(step)
        for i in range(NX):
            source = zn * NX + i

            @pl.when(source != acq)
            def _():
                slab_arrival(source).wait_recv()

            @pl.when(source == acq)
            def _():
                self_copy.wait()

            widen(source)
        pair_sums(zn, 0)
        for gap in (1, 2, 3):

            def side(s, c):
                za = jnp.where(s == 0, zn - gap, zn)
                other = jnp.where(s == 0, zn - gap, zn + gap)
                place = z_position(lax.rem(other - z + 2 * NZ, NZ))

                @pl.when((other >= 0) & (other < NZ) & (place < step))
                def _():
                    pair_sums(za, gap)

                return c

            lax.fori_loop(0, 2, side, 0)
        return carry

    lax.fori_loop(0, NZ, arrival, 0)

    top_lane = (lane & 64) == 0
    mid_lane = (lane & 32) == 0
    s1 = (sublane & 2) == 0
    s0 = (sublane & 1) == 0

    def gather_group(part, group):
        v = [sums[part, group * 8 + i] for i in range(8)]

        def fold_part(a, b):
            return jnp.where(upper, a, b) + pltpu.roll(jnp.where(upper, b, a), 4, 0)

        v = [fold_part(v[i], v[i + 4]) for i in range(4)]

        def fold_top(a, b):
            return jnp.where(top_lane, a, b) + pltpu.roll(jnp.where(top_lane, b, a), 64, 1)

        v = [fold_top(v[i], v[i + 2]) for i in range(2)]
        a, b = v
        w = jnp.where(mid_lane, a + pltpu.roll(a, 96, 1), b + pltpu.roll(b, 32, 1))
        u = pltpu.roll(w, 64, 1)
        w = jnp.where(
            s1 == top_lane, w, jnp.where(s1, pltpu.roll(u, 6, 0), pltpu.roll(u, 2, 0))
        )
        w = jnp.where(
            s0 == mid_lane,
            w,
            jnp.where(
                s0,
                pltpu.roll(pltpu.roll(w, 32, 1), 7, 0),
                pltpu.roll(pltpu.roll(w, 96, 1), 1, 0),
            ),
        )
        dense[part, pl.ds(pl.multiple_of(group * 8, 8), 8), :] = w

    def gather_both(group, c):
        gather_group(0, group)
        gather_group(1, group)
        return c

    lax.fori_loop(0, 40, gather_both, 0)

    def gather_power(group, c):
        gather_group(0, group)
        return c

    lax.fori_loop(40, 44, gather_power, 0)

    for part in range(2):
        for h in range(3):
            flipped = dense[part, h * 128 : (h + 1) * 128, :].T
            for lr in range(4):
                message[h, pl.ds(part * 4 + lr, 32, stride=8), :] = flipped[
                    lr * 32 : (lr + 1) * 32, :
                ]

    own_look = x * 8 + band
    own_source = band * NX + x

    def message_copy(look):
        return pltpu.make_async_remote_copy(
            src_ref=message.at[:, pl.ds(pl.multiple_of(look * 8, 8), 8), :],
            dst_ref=received.at[own_source],
            send_sem=send2_sem.at[look],
            recv_sem=recv2_sem.at[own_source],
            device_id=(z * NX + look // 8, lax.rem(look, 8)),
            device_id_type=MESH,
        )

    def send_message(s, c):
        message_copy(lax.rem(own_look + s, ACQ)).start()
        return c

    lax.fori_loop(1, ACQ, send_message, 0)
    for h in range(3):
        received[own_source, h] = message[h, pl.ds(pl.multiple_of(own_look * 8, 8), 8), :]

    def valid_arrival(s, c):
        i = lax.rem(acq + s, ACQ)
        pltpu.make_async_remote_copy(
            src_ref=own_valid,
            dst_ref=all_valid.at[i],
            send_sem=vsend_sem.at[i],
            recv_sem=vrecv_sem.at[i],
            device_id=(i, band),
            device_id_type=MESH,
        ).wait()
        return c

    lax.fori_loop(1, ACQ, valid_arrival, 0)
    all_valid[acq] = own_valid[...]

    for n in range(NZ):
        for g in range(NX):

            @pl.when(z_at(send_step(n)) * NX + g != acq)
            def _():
                slab_copy(n, g).wait_send()

    def message_arrival(s, c):
        look = lax.rem(own_look + s, ACQ)
        message_copy(look).wait_send()
        source = lax.rem(own_source + s, ACQ)
        pltpu.make_async_remote_copy(
            src_ref=message.at[:, pl.ds(0, 8), :],
            dst_ref=received.at[source],
            send_sem=send2_sem.at[0],
            recv_sem=recv2_sem.at[source],
            device_id=(acq, band),
            device_id_type=MESH,
        ).wait_recv()
        return c

    lax.fori_loop(1, ACQ, message_arrival, 0)

    final = [[], []]
    for h in range(3):
        parts = [[], []]
        for s in range(0, ACQ, 2):
            a = received[s, h]
            b = received[s + 1, h]
            parts[0].append(jnp.where(upper, a, pltpu.roll(b, 4, 0)))
            parts[1].append(jnp.where(upper, pltpu.roll(a, 4, 0), b))
        for part in range(2):
            final[part].append(jnp.concatenate(parts[part], axis=0).T)

    power[...] = jnp.ones_like(power)
    power[0:ACQ, :] = final[0][2][64:96, :] * (1.0 / CELLS) + EPS
    valid = all_valid[...].reshape(ACQ, 128)
    position = lax.broadcasted_iota(jnp.int32, (ACQ, 128), 0)
    for k in range(1, PARTNERS + 1):
        scale = lax.rsqrt(power[0:ACQ, :] * power[k : k + ACQ, :]) * (1.0 / CELLS)
        on = jnp.broadcast_to(valid[:, k - 1 : k], (ACQ, 128))
        weight = jnp.where(position + k < ACQ, scale * on, 0.0)
        h, at = divmod((k - 1) * ACQ, 128)
        for part in range(2):
            out_ref[part, pl.ds(k - 1, ACQ, stride=PARTNERS), :] = (
                final[part][h][at : at + ACQ, :] * weight
            )


def per_device(slc, validity):
    dma = pltpu.SemaphoreType.DMA
    out = pl.pallas_call(
        kernel,
        out_shape=jax.ShapeDtypeStruct((2, ACQ * PARTNERS, 128), F32),
        in_specs=[
            pl.BlockSpec(memory_space=pl.ANY),
            pl.BlockSpec(memory_space=pltpu.VMEM),
        ],
        out_specs=pl.BlockSpec(memory_space=pltpu.VMEM),
        scratch_shapes=[
            pltpu.VMEM((NZ, 2, 80, BLOCK), BF16),
            pltpu.VMEM((BLOCK, BLOCK), BF16),
            pltpu.VMEM((NZ, NX, SLAB, 128), BF16),
            pltpu.VMEM((ACQ, SLAB, 128), BF16),
            pltpu.VMEM((ACQ, SLAB, 128), F32),
            pltpu.VMEM((ACQ, SLAB, 128), F32),
            pltpu.VMEM((2, SUMS, 8, 128), F32),
            pltpu.VMEM((2, SUMS, 128), F32),
            pltpu.VMEM((3, 256, 128), F32),
            pltpu.VMEM((ACQ, 3, 8, 128), F32),
            pltpu.VMEM((1, 128), F32),
            pltpu.VMEM((ACQ, 1, 128), F32),
            pltpu.VMEM((48, 128), F32),
            dma((NZ,)),
            dma,
            dma((NZ, NX)),
            dma((ACQ,)),
            dma((ACQ,)),
            dma((ACQ,)),
            dma((ACQ,)),
            dma((ACQ,)),
        ],
        compiler_params=pltpu.CompilerParams(
            collective_id=0, has_side_effects=True, vmem_limit_bytes=56 * 2**20
        ),
    )(slc, validity)
    return out.transpose(0, 2, 1)[:, :, None, :]


def solution(mesh):
    in_specs = (P(None, "acq", "rows", None), P("acq", None))
    out_specs = P(None, None, ("acq", "rows"), None)
    return jax.shard_map(
        per_device, mesh=mesh, in_specs=in_specs, out_specs=out_specs, check_vma=False
    )
```

time: 971 us -> 76.2 us (0.08)
  waiting for transfers between devices: 600 us -> 0 us
  blocking collectives: 127 us -> 0 us
  matrix products: 125 us -> 0 us
  Pallas kernels: 0 us -> 74.4 us
  local copies, waits for them, and re-layouts: 61 us -> 1.72 us
  loops' own time: 33 us -> 0 us
  starting transfers between devices: 18 us -> 0 us
    ppermute x10 -> x0, waiting for transfers between devices: 600 us -> none  [passed_along(): return lax.ppermute(array, axis, pairs)]
    all_to_all x2 -> x0, blocking collectives: 127 us -> none  [the longest x1 111 us: per_device(): lax.all_to_all(local, 'acq', split_axis=2, concat_axis=3, tiled=True)]
    dot_general x42 -> x0, matrix products: 125 us -> none  [the longest x21 109 us: box_mean(): jnp.dot(values.reshape(count * rows, cols), col_table, precision=lax.Prec...]
    pallas_call x0 -> x1, Pallas kernels: none -> 74.4 us  [per_device(): pl.pallas_call(kernel, out_shape=jax.ShapeDtypeStruct((2, ACQ * PARTNERS,...]
    another operation x1 -> x0, loops' own time: 33 us -> none  [coherence_block(): stacked = lax.map(one_offset, jnp.arange(1, PARTNERS + 1, dtype=jnp.int32))]
    unnamed x23 -> x1, local copies, waits for them, and re-layouts: 23.5 us -> 1.72 us
    ppermute x10 -> x0, starting transfers between devices: 18 us -> none  [passed_along(): return lax.ppermute(array, axis, pairs)]
    all_to_all x6 -> x0, local copies, waits for them, and re-layouts: 14 us -> none  [the longest x4 13.1 us: per_device(): lax.all_to_all(local, 'acq', split_axis=2, concat_axis=3, tiled=True)]
  transfers between devices with their start and end apart: 10 -> 0, of which waited for: 6 -> 0; matrix products, arithmetic and copies ran while one was open for 1% -> 0% of each run, Pallas kernels for 0% -> 0%
where the time goes in v1:
time: 76.2 us; the launch traced here: 76.1 us
  Pallas kernels  74.4 us (98%)
  local copies, waits for them, and re-layouts  1.72 us (2%)
    pallas_call x1, Pallas kernels, per_device(): pl.pallas_call(kernel, out_shape=jax.ShapeDtypeStruct((2, ACQ * PARTNERS,...  74.4 us
    unnamed x1, local copies, waits for them, and re-layouts  1.72 us

profile of v1, /device:TPU:33, one launch (start us, length us, event | category | flops | bytes accessed | tf_op | source)
XLA Modules:
  0.0 76.1 jit_solution(16064280656795472391)
XLA Ops:
  0.0 74.4 %shard_map.28 = f32[2,320,128]{2,1,0:T(8,128)} custom-call(bf16[2,1,80,5120]{3,2,1,0:T(8,128)(2,1)} %slc_ref.1, s32[1,10]{1,0:T(1,128)} %validity_ref.1), custom_call_target="tpu_custom_call" | custom-call | tf_op jit(solution)/shard_map/pallas_call | solution.py:398
  74.4 1.7 %copy.5 = f32[2,128,1,320]{1,3,2,0:T(8,128)} copy(f32[2,128,1,320]{1,3,2,0:T(8,128)} %bitcast.5) | data formatting | bytes 655360

commit v2 on v1

--- a/solution.py
+++ b/solution.py
@@ -140,6 +140,12 @@
     prepare(0)
     pl.semaphore_wait(barrier, 59)
 
+    def send_valid(s, c):
+        valid_copy(lax.rem(acq + s, ACQ)).start()
+        return c
+
+    lax.fori_loop(1, ACQ, send_valid, 0)
+
     def prepare_and_send(n, c):
         send(n - 1)
         prepare(n)
@@ -148,12 +154,6 @@
     lax.fori_loop(1, NZ, prepare_and_send, 0)
     send(NZ - 1)
     self_copy.start()
-
-    def send_valid(s, c):
-        valid_copy(lax.rem(acq + s, ACQ)).start()
-        return c
-
-    lax.fori_loop(1, ACQ, send_valid, 0)
 
     for part in range(2):
         for k in range(1, PARTNERS + 1):
@@ -173,6 +173,18 @@
             device_id=(acq, band),
             device_id_type=MESH,
         )
+
+    def valid_arrival(i):
+        pltpu.make_async_remote_copy(
+            src_ref=own_valid,
+            dst_ref=all_valid.at[i],
+            send_sem=vsend_sem.at[i],
+            recv_sem=vrecv_sem.at[i],
+            device_id=(i, band),
+            device_id_type=MESH,
+        ).wait()
+
+    all_valid[acq] = own_valid[...]
 
     def widen(i):
         for t in range(25):
@@ -227,6 +239,7 @@
 
             @pl.when(source != acq)
             def _():
+                valid_arrival(source)
                 slab_arrival(source).wait_recv()
 
             @pl.when(source == acq)
@@ -285,20 +298,19 @@
                 pltpu.roll(pltpu.roll(w, 96, 1), 1, 0),
             ),
         )
-        dense[part, pl.ds(pl.multiple_of(group * 8, 8), 8), :] = w
-
-    def gather_both(group, c):
-        gather_group(0, group)
-        gather_group(1, group)
-        return c
-
-    lax.fori_loop(0, 40, gather_both, 0)
-
-    def gather_power(group, c):
-        gather_group(0, group)
-        return c
-
-    lax.fori_loop(40, 44, gather_power, 0)
+        return w
+
+    def gather_batch(which):
+        values = [gather_group(part, group) for part, group in which]
+        for (part, group), value in zip(which, values):
+            dense[part, pl.ds(pl.multiple_of(group * 8, 8), 8), :] = value
+
+    def gather_both(batch, c):
+        gather_batch([(part, batch * 5 + i) for part in range(2) for i in range(5)])
+        return c
+
+    lax.fori_loop(0, 8, gather_both, 0)
+    gather_batch([(0, 40 + i) for i in range(4)])
 
     for part in range(2):
         for h in range(3):
@@ -328,21 +340,6 @@
     lax.fori_loop(1, ACQ, send_message, 0)
     for h in range(3):
         received[own_source, h] = message[h, pl.ds(pl.multiple_of(own_look * 8, 8), 8), :]
-
-    def valid_arrival(s, c):
-        i = lax.rem(acq + s, ACQ)
-        pltpu.make_async_remote_copy(
-            src_ref=own_valid,
-            dst_ref=all_valid.at[i],
-            send_sem=vsend_sem.at[i],
-            recv_sem=vrecv_sem.at[i],
-            device_id=(i, band),
-            device_id_type=MESH,
-        ).wait()
-        return c
-
-    lax.fori_loop(1, ACQ, valid_arrival, 0)
-    all_valid[acq] = own_valid[...]
 
     for n in range(NZ):
         for g in range(NX):

time: 76.2 us -> 66.9 us (0.88)
  Pallas kernels: 74.4 us -> 65 us
    pallas_call x1, Pallas kernels: 74.4 us -> 65 us  [per_device(): pl.pallas_call(kernel, out_shape=jax.ShapeDtypeStruct((2, ACQ * PARTNERS,...]
where the time goes in v2:
time: 66.9 us; the launch traced here: 66.8 us
  Pallas kernels  65 us (97%)
  local copies, waits for them, and re-layouts  1.72 us (3%)
    pallas_call x1, Pallas kernels, per_device(): pl.pallas_call(kernel, out_shape=jax.ShapeDtypeStruct((2, ACQ * PARTNERS,...  65 us
    unnamed x1, local copies, waits for them, and re-layouts  1.72 us

profile of v2, /device:TPU:33, one launch (start us, length us, event | category | flops | bytes accessed | tf_op | source)
XLA Modules:
  0.0 66.8 jit_solution(48441503631260578)
XLA Ops:
  0.0 65.0 %shard_map.28 = f32[2,320,128]{2,1,0:T(8,128)} custom-call(bf16[2,1,80,5120]{3,2,1,0:T(8,128)(2,1)} %slc_ref.1, s32[1,10]{1,0:T(1,128)} %validity_ref.1), custom_call_target="tpu_custom_call" | custom-call | tf_op jit(solution)/shard_map/pallas_call | solution.py:395
  65.0 1.7 %copy.5 = f32[2,128,1,320]{1,3,2,0:T(8,128)} copy(f32[2,128,1,320]{1,3,2,0:T(8,128)} %bitcast.5) | data formatting | bytes 655360

commit v3 on v2

v3 whole, which is shorter than its diff:
```python
import jax
import jax.numpy as jnp
from jax import lax
from jax.sharding import PartitionSpec as P
from jax.experimental import pallas as pl
from jax.experimental.pallas import tpu as pltpu

PARTNERS = 10
EPS = 1e-06
CELLS = 100.0
ACQ = 32
NX = 4
NZ = 8
BLOCK = 640
CUT = 160
SLAB = 200
PAIRS_Z = NX * PARTNERS
POWER_AT = 2 * PAIRS_Z
SUMS = 88
MESH = pl.DeviceIdType.MESH
F32 = jnp.float32
BF16 = jnp.bfloat16


def z_offset(step):
    half = (step + 1) // 2
    return jnp.where(step % 2 == 1, half, lax.rem(NZ - half, NZ))


def z_position(offset):
    return jnp.where(offset <= 4, jnp.maximum(2 * offset - 1, 0), 2 * (NZ - offset))


def row_table():
    pieces = []
    for g in range(NX):
        q = lax.broadcasted_iota(jnp.int32, (40, 160), 0)
        take = ((q >> 2) & 1) * 80 + (4 * g + (q & 3)) * 5 + (q >> 3)
        pieces.append((lax.broadcasted_iota(jnp.int32, (40, 160), 1) == take).astype(F32))
    return jnp.concatenate(pieces, axis=0).astype(BF16)


def column_table():
    c = lax.broadcasted_iota(jnp.int32, (BLOCK, BLOCK), 1)
    take = (c & 31) * 20 + (c >> 7) * 4 + ((c >> 5) & 3)
    return (lax.broadcasted_iota(jnp.int32, (BLOCK, BLOCK), 0) == take).astype(F32).astype(BF16)


def kernel(
    slc_ref, validity_ref, out_ref,
    image, table, outgoing, arrived, lead, turned, sums, dense, message, received,
    final, weight, own_valid, all_valid, power,
    z_sem, plane_sem, in_sem, self_sem, send_sem, recv_sem, last_sem, vsend_sem, vrecv_sem, send2_sem, recv2_sem,
):
    acq = lax.axis_index("acq")
    band = lax.axis_index("rows")
    z = acq // NX
    x = lax.rem(acq, NX)

    def z_at(step):
        return lax.rem(z + z_offset(step), NZ)

    def load_block(n):
        at = pl.multiple_of(z_at(n) * BLOCK, 128)
        return pltpu.make_async_copy(
            slc_ref.at[:, 0, :, pl.ds(at, BLOCK)], image.at[n], in_sem.at[n]
        )

    for n in range(NZ):
        load_block(n).start()

    barrier = pltpu.get_barrier_semaphore()
    along_z = [(lax.rem(z + d, NZ) * NX + x, band) for d in (1, NZ - 1)]
    along_x = [(z * NX + lax.rem(x + d, NX), band) for d in (1, 2, 3)]
    bands = [(acq, lax.rem(band + d, 8)) for d in (2, 6)]
    bands.append((acq, band + 1 - 2 * lax.rem(band, 2)))

    def tell(semaphore, devices):
        for device in devices:
            pl.semaphore_signal(semaphore, inc=1, device_id=device, device_id_type=MESH)

    tell(barrier, along_x + along_z + bands)

    own_valid[...] = jnp.zeros_like(own_valid)
    own_valid[:, 0:PARTNERS] = (validity_ref[...] > 0).astype(F32)
    rows = row_table()
    table[...] = column_table()

    def prepare(n):
        load_block(n).wait()
        block = image[n].reshape(160, BLOCK)
        ordered = jnp.dot(rows, block, preferred_element_type=F32).astype(BF16)
        slab = jnp.dot(ordered, table[...], preferred_element_type=F32).astype(BF16)
        for g in range(NX):
            for c in range(5):
                outgoing[n * NX + g, c * 40 : (c + 1) * 40, :] = slab[
                    g * 40 : (g + 1) * 40, c * 128 : (c + 1) * 128
                ]

    def slab_copy(n, g, at, recv):
        return pltpu.make_async_remote_copy(
            src_ref=outgoing.at[n * NX + g, at, :],
            dst_ref=arrived.at[acq, at, :],
            send_sem=send_sem,
            recv_sem=recv,
            device_id=(z_at(n) * NX + g, band),
            device_id_type=MESH,
        )

    whole = pl.ds(0, SLAB)
    first_rows = pl.ds(0, CUT)
    last_rows = pl.ds(CUT, SLAB - CUT)

    def valid_copy(to):
        return pltpu.make_async_remote_copy(
            src_ref=own_valid,
            dst_ref=all_valid.at[acq],
            send_sem=vsend_sem,
            recv_sem=vrecv_sem,
            device_id=(to, band),
            device_id_type=MESH,
        )

    self_copy = pltpu.make_async_copy(outgoing.at[x], arrived.at[acq], self_sem)

    def send(n):
        for g in range(NX):
            to = z_at(n) * NX + g

            @pl.when(to != acq)
            def _():
                valid_copy(to).start()
                slab_copy(n, g, whole, recv_sem.at[acq]).start()

    prepare(0)
    pl.semaphore_wait(barrier, 8)
    tell(z_sem.at[0], along_z)
    tell(plane_sem.at[0], bands)
    send(0)
    self_copy.start()

    def ring(d, c):
        pl.semaphore_wait(z_sem.at[d - 1], 2)
        tell(z_sem.at[d], along_z)
        prepare(2 * d - 1)
        send(2 * d - 1)
        pl.semaphore_wait(plane_sem.at[d - 1], 3)

        @pl.when(d < 3)
        def _():
            tell(plane_sem.at[d], bands)

        prepare(2 * d)
        send(2 * d)
        return c

    lax.fori_loop(1, 4, ring, 0)
    pl.semaphore_wait(z_sem.at[3], 2)
    prepare(NZ - 1)
    for g in range(NX):
        valid_copy(z_at(NZ - 1) * NX + g).start()
        slab_copy(NZ - 1, g, first_rows, recv_sem.at[acq]).start()
    for g in range(NX):
        slab_copy(NZ - 1, g, last_rows, last_sem.at[x]).start()

    for a in range(ACQ - PARTNERS, ACQ):
        for part in range(2):
            at = part * PAIRS_Z + a % NX * PARTNERS
            sums[a // NX, at + ACQ - 1 - a : at + PARTNERS] = jnp.zeros(
                (a - ACQ + PARTNERS + 1, 8, 128), F32
            )
    sums[:, POWER_AT + NX :] = jnp.zeros((NZ, SUMS - POWER_AT - NX, 8, 128), F32)
    dense[SUMS:, :] = jnp.zeros((128 - SUMS, 128), F32)

    sublane = lax.broadcasted_iota(jnp.int32, (8, 128), 0)
    lane = lax.broadcasted_iota(jnp.int32, (8, 128), 1)
    upper = sublane < 4
    sign = jnp.where(upper, -1.0, 1.0).astype(F32)

    def slab_arrival(i, at, recv):
        return pltpu.make_async_remote_copy(
            src_ref=outgoing.at[0, at, :],
            dst_ref=arrived.at[i, at, :],
            send_sem=send_sem,
            recv_sem=recv,
            device_id=(acq, band),
            device_id_type=MESH,
        )

    all_valid[acq] = own_valid[...]

    def widen(i, begin, end):
        for t in range(begin // 8, end // 8):
            at = pl.ds(t * 8, 8)
            value = arrived[i, at, :].astype(F32)
            lead[i, at, :] = value
            turned[i, at, :] = pltpu.roll(value, 4, 0) * sign

    def pair_sums(za, gap, begin=0, end=SLAB):
        pairs = [
            (xa, xb)
            for xa in range(NX)
            for xb in range(NX)
            if 1 <= gap * NX + xb - xa <= PARTNERS
        ]
        powers = range(NX) if gap == 0 else ()

        def body(c, carry):
            carry = list(carry)
            for r in range(5):
                at = pl.ds(pl.multiple_of(c * 40 + r * 8, 8), 8)
                first = [lead[za * NX + i, at, :] for i in range(NX)]
                later = [lead[(za + gap) * NX + i, at, :] for i in range(NX)]
                later_turned = [turned[(za + gap) * NX + i, at, :] for i in range(NX)]
                m = 0
                for xa, xb in pairs:
                    carry[m] = carry[m] + first[xa] * later[xb]
                    carry[m + 1] = carry[m + 1] + first[xa] * later_turned[xb]
                    m += 2
                for i in powers:
                    carry[m] = carry[m] + first[i] * first[i]
                    m += 1
            return tuple(carry)

        slots = []
        for xa, xb in pairs:
            slot = xa * PARTNERS + gap * NX + xb - xa - 1
            slots += [slot, PAIRS_Z + slot]
        slots += [POWER_AT + i for i in powers]
        if begin:
            total = tuple(sums[za, slot] for slot in slots)
        else:
            total = (jnp.zeros((8, 128), F32),) * len(slots)
        total = lax.fori_loop(begin // 40, end // 40, body, total)
        for slot, value in zip(slots, total):
            sums[za, slot] = value

    def plane_sums(step, begin=0, end=SLAB):
        zn = z_at(step)
        pair_sums(zn, 0, begin, end)
        for gap in (1, 2, 3):

            def side(s, c):
                za = jnp.where(s == 0, zn - gap, zn)
                other = jnp.where(s == 0, zn - gap, zn + gap)
                place = z_position(lax.rem(other - z + 2 * NZ, NZ))

                @pl.when((other >= 0) & (other < NZ) & (place < step))
                def _():
                    pair_sums(za, gap, begin, end)

                return c

            lax.fori_loop(0, 2, side, 0)

    def arrival(step, carry):
        for i in range(NX):
            source = z_at(step) * NX + i

            @pl.when(source != acq)
            def _():
                slab_arrival(source, whole, recv_sem.at[source]).wait_recv()

            @pl.when(source == acq)
            def _():
                self_copy.wait()

            widen(source, 0, SLAB)
        plane_sums(step)
        return carry

    def last_arrival():
        plane = z_at(NZ - 1) * NX
        for i in range(NX):
            slab_arrival(plane + i, first_rows, recv_sem.at[plane + i]).wait_recv()
            widen(plane + i, 0, CUT)
        plane_sums(NZ - 1, 0, CUT)
        for i in range(NX):
            slab_arrival(plane + i, last_rows, last_sem.at[i]).wait_recv()
            widen(plane + i, CUT, SLAB)
        plane_sums(NZ - 1, CUT, SLAB)

    top_lane = (lane & 64) == 0
    mid_lane = (lane & 32) == 0
    s1 = (sublane & 2) == 0
    s0 = (sublane & 1) == 0

    def gather_group(za, group):
        v = [sums[za, group * 8 + i] for i in range(8)]

        def fold_part(a, b):
            return jnp.where(upper, a, b) + pltpu.roll(jnp.where(upper, b, a), 4, 0)

        v = [fold_part(v[i], v[i + 4]) for i in range(4)]

        def fold_top(a, b):
            return jnp.where(top_lane, a, b) + pltpu.roll(jnp.where(top_lane, b, a), 64, 1)

        v = [fold_top(v[i], v[i + 2]) for i in range(2)]
        a, b = v
        w = jnp.where(mid_lane, a + pltpu.roll(a, 96, 1), b + pltpu.roll(b, 32, 1))
        u = pltpu.roll(w, 64, 1)
        w = jnp.where(
            s1 == top_lane, w, jnp.where(s1, pltpu.roll(u, 6, 0), pltpu.roll(u, 2, 0))
        )
        w = jnp.where(
            s0 == mid_lane,
            w,
            jnp.where(
                s0,
                pltpu.roll(pltpu.roll(w, 32, 1), 7, 0),
                pltpu.roll(pltpu.roll(w, 96, 1), 1, 0),
            ),
        )
        return w

    def fill_message(q):
        def half(i, c):
            za = lax.rem(z + 2 * q + i + NZ - 3, NZ)
            values = [gather_group(za, group) for group in range(SUMS // 8)]
            for group, value in enumerate(values):
                dense[group * 8 : group * 8 + 8, :] = value
            flipped = dense[...].T
            for lr in range(4):
                message[q, pl.ds(i * 4 + lr, 32, stride=8), :] = flipped[
                    lr * 32 : (lr + 1) * 32, :
                ]
            return c

        lax.fori_loop(0, 2, half, 0)

    own_look = x * 8 + band
    own_source = band * NX + x

    def message_rows(look):
        return pl.ds(pl.multiple_of(look * 8, 8), 8)

    def message_copy(q, look):
        return pltpu.make_async_remote_copy(
            src_ref=message.at[q, message_rows(look), :],
            dst_ref=received.at[q, own_source],
            send_sem=send2_sem.at[q],
            recv_sem=recv2_sem.at[q],
            device_id=(z * NX + look // 8, lax.rem(look, 8)),
            device_id_type=MESH,
        )

    def send_message(q):
        def one(s, c):
            message_copy(q, lax.rem(own_look + s, ACQ)).start()
            return c

        lax.fori_loop(1, ACQ, one, 0)
        received[q, own_source] = message[q, message_rows(own_look), :]

    lax.fori_loop(0, NZ - 1, arrival, 0)
    for q in (0, 1):
        fill_message(q)
        send_message(q)
    last_arrival()
    for q in (2, 3):
        fill_message(q)
        send_message(q)

    valid_group = all_valid.at[pl.ds(0, ACQ - 1)]
    pltpu.make_async_copy(valid_group, valid_group, vrecv_sem).wait()
    pltpu.make_async_copy(valid_group, valid_group, vsend_sem).wait()
    slab_group = outgoing.at[pl.ds(0, ACQ - 1)]
    pltpu.make_async_copy(slab_group, slab_group, send_sem).wait()

    valid = all_valid[...].reshape(ACQ, 128)
    by_partner = jnp.concatenate([valid, jnp.zeros((96, 128), F32)], axis=0).T
    partner = lax.broadcasted_iota(jnp.int32, (16, 128), 0)
    for a in range(ACQ):
        on = jnp.broadcast_to(by_partner[0:16, a : a + 1], (16, 128)) * (1.0 / CELLS)
        on = jnp.where(partner < ACQ - 1 - a, on, 0.0)
        weight[a * PARTNERS : a * PARTNERS + PARTNERS, :] = on[0:PARTNERS, :]

    for q in range(4):
        group = received.at[q, pl.ds(0, ACQ - 1)]
        pltpu.make_async_copy(group, group, recv2_sem.at[q]).wait()
        pltpu.make_async_copy(group, group, send2_sem.at[q]).wait()
        halves = [[], []]
        for s in range(0, ACQ, 2):
            a = received[q, s]
            b = received[q, s + 1]
            halves[0].append(jnp.where(upper, a, pltpu.roll(b, 4, 0)))
            halves[1].append(jnp.where(upper, pltpu.roll(a, 4, 0), b))
        for i in range(2):
            za = lax.rem(z + 2 * q + i + NZ - 3, NZ)
            final[za] = jnp.concatenate(halves[i], axis=0).T[0:SUMS, :]

    power[...] = jnp.ones_like(power)
    for za in range(NZ):
        power[za * NX : za * NX + NX, :] = (
            final[za, POWER_AT : POWER_AT + NX, :] * (1.0 / CELLS) + EPS
        )
    for a in range(ACQ):
        at = a * PARTNERS
        pair_power = power[a : a + 1, :] * power[a + 1 : a + 1 + PARTNERS, :]
        weight[at : at + PARTNERS, :] = weight[at : at + PARTNERS, :] * lax.rsqrt(pair_power)
    for za in range(NZ):
        at = za * PAIRS_Z
        scale = weight[at : at + PAIRS_Z, :]
        for part in range(2):
            out_ref[part, at : at + PAIRS_Z, :] = (
                final[za, part * PAIRS_Z : (part + 1) * PAIRS_Z, :] * scale
            )


def per_device(slc, validity):
    dma = pltpu.SemaphoreType.DMA
    out = pl.pallas_call(
        kernel,
        out_shape=jax.ShapeDtypeStruct((2, ACQ * PARTNERS, 128), F32),
        in_specs=[
            pl.BlockSpec(memory_space=pl.ANY),
            pl.BlockSpec(memory_space=pltpu.VMEM),
        ],
        out_specs=pl.BlockSpec(memory_space=pltpu.VMEM),
        scratch_shapes=[
            pltpu.VMEM((NZ, 2, 80, BLOCK), BF16),
            pltpu.VMEM((BLOCK, BLOCK), BF16),
            pltpu.VMEM((ACQ, SLAB, 128), BF16),
            pltpu.VMEM((ACQ, SLAB, 128), BF16),
            pltpu.VMEM((ACQ, SLAB, 128), F32),
            pltpu.VMEM((ACQ, SLAB, 128), F32),
            pltpu.VMEM((NZ, SUMS, 8, 128), F32),
            pltpu.VMEM((128, 128), F32),
            pltpu.VMEM((4, 256, 128), F32),
            pltpu.VMEM((4, ACQ, 8, 128), F32),
            pltpu.VMEM((NZ, SUMS, 128), F32),
            pltpu.VMEM((ACQ * PARTNERS, 128), F32),
            pltpu.VMEM((1, 128), F32),
            pltpu.VMEM((ACQ, 1, 128), F32),
            pltpu.VMEM((48, 128), F32),
            pltpu.SemaphoreType.REGULAR((4,)),
            pltpu.SemaphoreType.REGULAR((3,)),
            dma((NZ,)),
            dma,
            dma,
            dma((ACQ,)),
            dma((NX,)),
            dma,
            dma,
            dma((4,)),
            dma((4,)),
        ],
        compiler_params=pltpu.CompilerParams(
            collective_id=0, has_side_effects=True, vmem_limit_bytes=56 * 2**20
        ),
    )(slc, validity)
    return out.transpose(0, 2, 1)[:, :, None, :]


def solution(mesh):
    in_specs = (P(None, "acq", "rows", None), P("acq", None))
    out_specs = P(None, None, ("acq", "rows"), None)
    return jax.shard_map(
        per_device, mesh=mesh, in_specs=in_specs, out_specs=out_specs, check_vma=False
    )
```

time: 66.9 us -> 65.6 us (0.981)
  Pallas kernels: 65 us -> 63.7 us
    pallas_call x1, Pallas kernels: 65 us -> 63.7 us  [per_device(): pl.pallas_call(kernel, out_shape=jax.ShapeDtypeStruct((2, ACQ * PARTNERS,...]
where the time goes in v3:
time: 65.6 us; the launch traced here: 65.4 us
  Pallas kernels  63.7 us (97%)
  local copies, waits for them, and re-layouts  1.72 us (3%)
    pallas_call x1, Pallas kernels, per_device(): pl.pallas_call(kernel, out_shape=jax.ShapeDtypeStruct((2, ACQ * PARTNERS,...  63.7 us
    unnamed x1, local copies, waits for them, and re-layouts  1.72 us

profile of v3, /device:TPU:33, one launch (start us, length us, event | category | flops | bytes accessed | tf_op | source)
XLA Modules:
  0.0 65.4 jit_solution(1688109674314175497)
XLA Ops:
  0.0 63.7 %shard_map.28 = f32[2,320,128]{2,1,0:T(8,128)} custom-call(bf16[2,1,80,5120]{3,2,1,0:T(8,128)(2,1)} %slc_ref.1, s32[1,10]{1,0:T(1,128)} %validity_ref.1), custom_call_target="tpu_custom_call" | custom-call | tf_op jit(solution)/shard_map/pallas_call | solution.py:413
  63.7 1.7 %copy.5 = f32[2,128,1,320]{1,3,2,0:T(8,128)} copy(f32[2,128,1,320]{1,3,2,0:T(8,128)} %bitcast.5) | data formatting | bytes 655360

commit v4 on v3

--- a/solution.py
+++ b/solution.py
@@ -170,7 +170,7 @@
                 (a - ACQ + PARTNERS + 1, 8, 128), F32
             )
     sums[:, POWER_AT + NX :] = jnp.zeros((NZ, SUMS - POWER_AT - NX, 8, 128), F32)
-    dense[SUMS:, :] = jnp.zeros((128 - SUMS, 128), F32)
+    dense[NZ * SUMS :, :] = jnp.zeros((768 - NZ * SUMS, 128), F32)
 
     sublane = lax.broadcasted_iota(jnp.int32, (8, 128), 0)
     lane = lax.broadcasted_iota(jnp.int32, (8, 128), 1)
@@ -314,20 +314,19 @@
         )
         return w
 
-    def fill_message(q):
-        def half(i, c):
-            za = lax.rem(z + 2 * q + i + NZ - 3, NZ)
-            values = [gather_group(za, group) for group in range(SUMS // 8)]
-            for group, value in enumerate(values):
-                dense[group * 8 : group * 8 + 8, :] = value
-            flipped = dense[...].T
-            for lr in range(4):
-                message[q, pl.ds(i * 4 + lr, 32, stride=8), :] = flipped[
-                    lr * 32 : (lr + 1) * 32, :
-                ]
-            return c
-
-        lax.fori_loop(0, 2, half, 0)
+    def gather(i, c):
+        za = lax.rem(z + i + NZ - 3, NZ)
+        values = [gather_group(za, group) for group in range(SUMS // 8)]
+        for group, value in enumerate(values):
+            dense[pl.ds(pl.multiple_of(i * SUMS + group * 8, 8), 8), :] = value
+        return c
+
+    def fill_message(tile):
+        flipped = dense[tile * 128 : tile * 128 + 128, :].T
+        for lr in range(4):
+            message[tile // 2, pl.ds(tile % 2 * 4 + lr, 32, stride=8), :] = flipped[
+                lr * 32 : (lr + 1) * 32, :
+            ]
 
     own_look = x * 8 + band
     own_source = band * NX + x
@@ -335,32 +334,31 @@
     def message_rows(look):
         return pl.ds(pl.multiple_of(look * 8, 8), 8)
 
-    def message_copy(q, look):
+    def message_copy(look):
         return pltpu.make_async_remote_copy(
-            src_ref=message.at[q, message_rows(look), :],
-            dst_ref=received.at[q, own_source],
-            send_sem=send2_sem.at[q],
-            recv_sem=recv2_sem.at[q],
+            src_ref=message.at[:, message_rows(look), :],
+            dst_ref=received.at[:, own_source],
+            send_sem=send2_sem,
+            recv_sem=recv2_sem,
             device_id=(z * NX + look // 8, lax.rem(look, 8)),
             device_id_type=MESH,
         )
 
-    def send_message(q):
-        def one(s, c):
-            message_copy(q, lax.rem(own_look + s, ACQ)).start()
-            return c
-
-        lax.fori_loop(1, ACQ, one, 0)
-        received[q, own_source] = message[q, message_rows(own_look), :]
+    def send_message(s, c):
+        message_copy(lax.rem(own_look + s, ACQ)).start()
+        return c
 
     lax.fori_loop(0, NZ - 1, arrival, 0)
-    for q in (0, 1):
-        fill_message(q)
-        send_message(q)
+    lax.fori_loop(0, 4, gather, 0)
+    fill_message(0)
+    fill_message(1)
     last_arrival()
-    for q in (2, 3):
-        fill_message(q)
-        send_message(q)
+    lax.fori_loop(4, NZ, gather, 0)
+    for tile in range(2, 6):
+        fill_message(tile)
+    lax.fori_loop(1, ACQ, send_message, 0)
+    for h in range(3):
+        received[h, own_source] = message[h, message_rows(own_look), :]
 
     valid_group = all_valid.at[pl.ds(0, ACQ - 1)]
     pltpu.make_async_copy(valid_group, valid_group, vrecv_sem).wait()
@@ -376,19 +374,22 @@
         on = jnp.where(partner < ACQ - 1 - a, on, 0.0)
         weight[a * PARTNERS : a * PARTNERS + PARTNERS, :] = on[0:PARTNERS, :]
 
-    for q in range(4):
-        group = received.at[q, pl.ds(0, ACQ - 1)]
-        pltpu.make_async_copy(group, group, recv2_sem.at[q]).wait()
-        pltpu.make_async_copy(group, group, send2_sem.at[q]).wait()
+    group = received.at[:, pl.ds(0, ACQ - 1)]
+    pltpu.make_async_copy(group, group, recv2_sem).wait()
+    pltpu.make_async_copy(group, group, send2_sem).wait()
+    for h in range(3):
         halves = [[], []]
         for s in range(0, ACQ, 2):
-            a = received[q, s]
-            b = received[q, s + 1]
+            a = received[h, s]
+            b = received[h, s + 1]
             halves[0].append(jnp.where(upper, a, pltpu.roll(b, 4, 0)))
             halves[1].append(jnp.where(upper, pltpu.roll(a, 4, 0), b))
         for i in range(2):
-            za = lax.rem(z + 2 * q + i + NZ - 3, NZ)
-            final[za] = jnp.concatenate(halves[i], axis=0).T[0:SUMS, :]
+            dense[h * 256 + i * 128 : h * 256 + i * 128 + 128, :] = jnp.concatenate(
+                halves[i], axis=0
+            ).T
+    for i in range(NZ):
+        final[lax.rem(z + i + NZ - 3, NZ)] = dense[i * SUMS : (i + 1) * SUMS, :]
 
     power[...] = jnp.ones_like(power)
     for za in range(NZ):
@@ -426,9 +427,9 @@
             pltpu.VMEM((ACQ, SLAB, 128), F32),
             pltpu.VMEM((ACQ, SLAB, 128), F32),
             pltpu.VMEM((NZ, SUMS, 8, 128), F32),
-            pltpu.VMEM((128, 128), F32),
-            pltpu.VMEM((4, 256, 128), F32),
-            pltpu.VMEM((4, ACQ, 8, 128), F32),
+            pltpu.VMEM((768, 128), F32),
+            pltpu.VMEM((3, 256, 128), F32),
+            pltpu.VMEM((3, ACQ, 8, 128), F32),
             pltpu.VMEM((NZ, SUMS, 128), F32),
             pltpu.VMEM((ACQ * PARTNERS, 128), F32),
             pltpu.VMEM((1, 128), F32),
@@ -443,8 +444,8 @@
             dma((NX,)),
             dma,
             dma,
-            dma((4,)),
-            dma((4,)),
+            dma,
+            dma,
         ],
         compiler_params=pltpu.CompilerParams(
             collective_id=0, has_side_effects=True, vmem_limit_bytes=56 * 2**20

time: 65.6 us -> 63.5 us (0.968)
  Pallas kernels: 63.7 us -> 61.6 us
    pallas_call x1, Pallas kernels: 63.7 us -> 61.6 us  [per_device(): pl.pallas_call(kernel, out_shape=jax.ShapeDtypeStruct((2, ACQ * PARTNERS,...]
where the time goes in v4:
time: 63.5 us; the launch traced here: 63.3 us
  Pallas kernels  61.6 us (97%)
  local copies, waits for them, and re-layouts  1.72 us (3%)
    pallas_call x1, Pallas kernels, per_device(): pl.pallas_call(kernel, out_shape=jax.ShapeDtypeStruct((2, ACQ * PARTNERS,...  61.6 us
    unnamed x1, local copies, waits for them, and re-layouts  1.72 us

profile of v4, /device:TPU:33, one launch (start us, length us, event | category | flops | bytes accessed | tf_op | source)
XLA Modules:
  0.0 63.3 jit_solution(1527728137097742726)
XLA Ops:
  0.0 61.6 %shard_map.28 = f32[2,320,128]{2,1,0:T(8,128)} custom-call(bf16[2,1,80,5120]{3,2,1,0:T(8,128)(2,1)} %slc_ref.1, s32[1,10]{1,0:T(1,128)} %validity_ref.1), custom_call_target="tpu_custom_call" | custom-call | tf_op jit(solution)/shard_map/pallas_call | solution.py:414
  61.6 1.7 %copy.5 = f32[2,128,1,320]{1,3,2,0:T(8,128)} copy(f32[2,128,1,320]{1,3,2,0:T(8,128)} %bitcast.5) | data formatting | bytes 655360
